TPU v7x, 32 devices: a whole 2x2x4 slice. The times are simulated.
32 devices in a mesh: px: 8 (over z, y), py: 4 (over x, core).
Axes of the slice: x: 2, y: 2, z: 4, core: 2. Of those that a mesh axis runs over, the one named last changes fastest.
Arguments:
- measured: float32 [256, 128, 128], P('px', 'py'), may hold values from -432 to 432, as said below
- spread_function: float32 [8, 8, 16], replicated, may hold values from 0.01 to 1
- smoothing: float32 [1], replicated, may hold values from 0.1 to 0.4
Outputs:
- solution_field: float32 [256, 128, 128], P('px', 'py')
- residual: float32 [256, 128, 128], P('px', 'py')
Inputs may be any that keep to these rules, and one draw needn't show every extreme that they name: measured is a float32 volume whose entries lie within the stated bounds.
All inputs are finite; a program needn't handle non-finite values.
Results may differ from a plain program's by a relative error of at most 0.0003.
Values sent between devices are 32-bit elements.
A program may use at most 128 MiB of HBM per device.

v0:
```python
import math

import jax
import jax.numpy as jnp
from jax import lax
from jax.sharding import PartitionSpec as P

ITERS = 5


highest = lax.Precision.HIGHEST
forms = ("jbc,jk->kbc", "ajc,jk->akc", "abj,jk->abk")


def with_halo(cells, sides, width, closed):
    for axis, dim in sides:
        count = lax.axis_size(axis)
        ends = count if closed else count - 1
        head = lax.slice_in_dim(cells, 0, width, axis=dim)
        tail = lax.slice_in_dim(cells, cells.shape[dim] - width, cells.shape[dim], axis=dim)
        cells = jnp.concatenate(
            [
                lax.ppermute(tail, axis, [(i, (i + 1) % count) for i in range(ends)]),
                cells,
                lax.ppermute(head, axis, [((i + 1) % count, i) for i in range(ends)]),
            ],
            axis=dim,
        )
    return cells


def contract(form, left, table):
    return jnp.einsum(form, left, table, precision=highest)


def dft_table(length):
    index = jnp.arange(length, dtype=jnp.int32)
    product = index[:, None] * index[None, :] % length
    angle = product.astype(jnp.float32) * (2.0 * math.pi / length)
    cosine = jnp.cos(angle)
    sine = jnp.sin(angle)
    return ((cosine, -sine), (cosine, sine))


def transform(real_part, imag_part, table, where):
    form = forms[where]
    cosine, sine = table
    new_real = contract(form, real_part, cosine) - contract(form, imag_part, sine)
    new_imag = contract(form, real_part, sine) + contract(form, imag_part, cosine)
    return (new_real, new_imag)


def phases(waves, count, length):
    offsets = jnp.arange(count, dtype=jnp.int32) - count // 2
    product = waves[:, None] * offsets[None, :] % length
    angle = product.astype(jnp.float32) * (2.0 * math.pi / length)
    return (jnp.cos(angle), -jnp.sin(angle))


def optical_transfer(kernel, waves_x, waves_y, waves_z, lengths):
    cos_x, sin_x = phases(waves_x, kernel.shape[0], lengths[0])
    cos_y, sin_y = phases(waves_y, kernel.shape[1], lengths[1])
    cos_z, sin_z = phases(waves_z, kernel.shape[2], lengths[2])
    first_real = jnp.einsum("abc,zc->abz", kernel, cos_z, precision=highest)
    first_imag = jnp.einsum("abc,zc->abz", kernel, sin_z, precision=highest)
    second_real = jnp.einsum("abz,yb->ayz", first_real, cos_y, precision=highest) - jnp.einsum(
        "abz,yb->ayz", first_imag, sin_y, precision=highest
    )
    second_imag = jnp.einsum("abz,yb->ayz", first_real, sin_y, precision=highest) + jnp.einsum(
        "abz,yb->ayz", first_imag, cos_y, precision=highest
    )
    third_real = jnp.einsum("ayz,xa->xyz", second_real, cos_x, precision=highest) - jnp.einsum(
        "ayz,xa->xyz", second_imag, sin_x, precision=highest
    )
    third_imag = jnp.einsum("ayz,xa->xyz", second_real, sin_x, precision=highest) + jnp.einsum(
        "ayz,xa->xyz", second_imag, cos_x, precision=highest
    )
    return (third_real, third_imag)


def spectral(source, tables, multiply, volume_cells):
    (forward_z, inverse_z), (forward_y, inverse_y), (forward_x, inverse_x) = tables
    real_part = contract(forms[2], source, forward_z[0])
    imag_part = contract(forms[2], source, forward_z[1])
    real_part, imag_part = transform(real_part, imag_part, forward_y, 1)
    real_part, imag_part = (
        lax.all_to_all(real_part, "py", split_axis=1, concat_axis=0, tiled=True),
        lax.all_to_all(imag_part, "py", split_axis=1, concat_axis=0, tiled=True),
    )
    real_part, imag_part = (
        lax.all_to_all(real_part, "px", split_axis=2, concat_axis=0, tiled=True),
        lax.all_to_all(imag_part, "px", split_axis=2, concat_axis=0, tiled=True),
    )
    real_part, imag_part = transform(real_part, imag_part, forward_x, 0)
    real_part, imag_part = multiply(real_part, imag_part)
    real_part, imag_part = transform(real_part, imag_part, inverse_x, 0)
    real_part, imag_part = (
        lax.all_to_all(real_part, "px", split_axis=0, concat_axis=2, tiled=True),
        lax.all_to_all(imag_part, "px", split_axis=0, concat_axis=2, tiled=True),
    )
    real_part, imag_part = (
        lax.all_to_all(real_part, "py", split_axis=0, concat_axis=1, tiled=True),
        lax.all_to_all(imag_part, "py", split_axis=0, concat_axis=1, tiled=True),
    )
    real_part, imag_part = transform(real_part, imag_part, inverse_y, 1)
    result = contract(forms[2], real_part, inverse_z[0]) - contract(
        forms[2], imag_part, inverse_z[1]
    )
    return result * (1.0 / volume_cells)


def stencil(volume, penalty):
    padded = with_halo(volume, ((("px", "py"), 0),), 1, False)
    padded = jnp.pad(padded, ((0, 0), (1, 1), (1, 1)))
    beside = padded[2:, 1:-1, 1:-1] + padded[:-2, 1:-1, 1:-1]
    beside = beside + padded[1:-1, 2:, 1:-1] + padded[1:-1, :-2, 1:-1]
    beside = beside + padded[1:-1, 1:-1, 2:] + padded[1:-1, 1:-1, :-2]
    return penalty * (6.0 * volume - beside)


def squares(residual):
    return lax.psum(jnp.sum(residual * residual), ("px", "py"))


def shards(measured, spread_function, smoothing):
    penalty = smoothing[0]
    local_x, local_y, planes = measured.shape
    groups_x = lax.axis_size("px")
    groups_y = lax.axis_size("py")
    lines_x = local_x * groups_x
    lines_y = local_y * groups_y
    volume_cells = lines_x * lines_y * planes
    tables = (dft_table(planes), dft_table(lines_y), dft_table(lines_x))
    kernel = spread_function / jnp.sum(spread_function)
    waves_x = jnp.arange(lines_x, dtype=jnp.int32)
    waves_y = lax.axis_index("py") * local_y + jnp.arange(local_y, dtype=jnp.int32)
    block_z = planes // groups_x
    waves_z = lax.axis_index("px") * block_z + jnp.arange(block_z, dtype=jnp.int32)
    source = lax.all_to_all(measured, "py", split_axis=0, concat_axis=1, tiled=True)
    transfer_real, transfer_imag = optical_transfer(
        kernel, waves_x, waves_y, waves_z, (lines_x, lines_y, planes)
    )
    power = transfer_real * transfer_real + transfer_imag * transfer_imag

    def by_adjoint(real_part, imag_part):
        return (
            real_part * transfer_real + imag_part * transfer_imag,
            imag_part * transfer_real - real_part * transfer_imag,
        )

    def by_power(real_part, imag_part):
        return (real_part * power, imag_part * power)

    def operate(volume):
        return spectral(volume, tables, by_power, volume_cells) + stencil(volume, penalty)

    right_side = spectral(source, tables, by_adjoint, volume_cells)
    solution_field = jnp.zeros_like(right_side)
    residual = right_side
    direction = right_side
    norm_now = squares(residual)
    for count in range(ITERS):
        image = operate(direction)
        alpha = norm_now / lax.psum(jnp.sum(direction * image), ("px", "py"))
        solution_field = solution_field + alpha * direction
        residual = residual - alpha * image
        fresh = squares(residual)
        direction = residual + fresh / norm_now * direction
        norm_now = fresh
    solution_field, residual = (
        lax.all_to_all(solution_field, "py", split_axis=1, concat_axis=0, tiled=True),
        lax.all_to_all(residual, "py", split_axis=1, concat_axis=0, tiled=True),
    )
    return (solution_field, residual)


def solution(mesh):
    return jax.shard_map(
        shards,
        mesh=mesh,
        in_specs=(P("px", "py", None), P(), P()),
        out_specs=(P("px", "py", None), P("px", "py", None)),
        check_vma=False,
    )
```

profile of v0, /device:TPU:0, one launch (start us, length us, event | category | flops | bytes accessed | tf_op | source)
XLA Modules:
  0.0 1486.5 jit_solution(7586637526383574741)
XLA Ops:
  8.3 5.4 all-to-all-done
  24.6 5.9 all-to-all-done.1
  43.6 6.7 all-to-all-start.2
  57.0 8.3 all-to-all-done.2
  103.2 5.1 all-to-all-start.5
  117.3 5.8 all-to-all-done.5
  135.5 6.6 all-to-all-done.7
  161.6 5.9 all-to-all-done.8
  182.6 5.9 all-to-all-done.9
  212.4 8.3 all-to-all-done.10
  260.9 5.6 all-to-all-start.13
  275.6 5.6 all-to-all-done.13
  320.8 6.8 all-to-all-start.16
  330.5 6.4 all-to-all-done.16
  343.4 42.1 %all-reduce.5 = (f32[]{:T(128)}, f32[]{:T(128)}) all-reduce(f32[]{:T(128)} %get-tuple-element.3, f32[]{:T(128)} %get-tuple-element.2), channel_id=1, replica_groups=mesh['px'=8,'py'=4] {'px','py'}, use_global_device_ids=true, to_apply=%region_2.3 | all-reduce | flops 2 | bytes 16 | tf_op jit(solution)/shard_map/psum | solution.py:122
  387.6 38.9 %psum.72 = f32[]{:T(128)} all-reduce(f32[]{:T(128)} %multiply_reduce_fusion.7), channel_id=1, replica_groups=mesh['px'=8,'py'=4] {'px','py'}, use_global_device_ids=true, to_apply=%region_6.7 | all-reduce | flops 1 | bytes 8 | tf_op jit(solution)/shard_map/psum | solution.py:122
  439.8 6.0 all-to-all-done.17
  458.0 5.1 all-to-all-start.18
  469.2 9.0 all-to-all-done.18
  520.0 6.4 all-to-all-start.21
  535.1 6.2 all-to-all-done.21
  580.8 7.0 all-to-all-start.24
  591.4 6.4 all-to-all-done.24
  606.3 42.1 %psum.73 = f32[]{:T(128)} all-reduce(f32[]{:T(128)} %get-tuple-element.28), channel_id=1, replica_groups=mesh['px'=8,'py'=4] {'px','py'}, use_global_device_ids=true, to_apply=%region_8.9 | all-reduce | flops 1 | bytes 8 | tf_op jit(solution)/shard_map/psum | solution.py:164
  651.4 38.7 %psum.74 = f32[]{:T(128)} all-reduce(f32[]{:T(128)} %get-tuple-element.10), channel_id=1, replica_groups=mesh['px'=8,'py'=4] {'px','py'}, use_global_device_ids=true, to_apply=%region_10.11 | all-reduce | flops 1 | bytes 8 | tf_op jit(solution)/shard_map/psum | solution.py:122
  703.2 6.0 all-to-all-done.25
  721.4 5.4 all-to-all-start.26
  732.9 9.0 all-to-all-done.26
  784.0 6.1 all-to-all-start.29
  798.9 5.7 all-to-all-done.29
  844.6 7.0 all-to-all-start.32
  855.2 6.4 all-to-all-done.32
  870.2 42.0 %psum.75 = f32[]{:T(128)} all-reduce(f32[]{:T(128)} %get-tuple-element.30), channel_id=1, replica_groups=mesh['px'=8,'py'=4] {'px','py'}, use_global_device_ids=true, to_apply=%region_12.13 | all-reduce | flops 1 | bytes 8 | tf_op jit(solution)/shard_map/psum | solution.py:164
  915.3 38.7 %psum.76 = f32[]{:T(128)} all-reduce(f32[]{:T(128)} %get-tuple-element.8), channel_id=1, replica_groups=mesh['px'=8,'py'=4] {'px','py'}, use_global_device_ids=true, to_apply=%region_14.15 | all-reduce | flops 1 | bytes 8 | tf_op jit(solution)/shard_map/psum | solution.py:122
  986.2 5.3 all-to-all-start.34
  998.7 7.9 all-to-all-done.34
  1052.4 6.4 all-to-all-start.37
  1113.8 6.8 all-to-all-start.40
  1124.2 6.4 all-to-all-done.40
  1139.2 42.0 %psum.77 = f32[]{:T(128)} all-reduce(f32[]{:T(128)} %get-tuple-element.32), channel_id=1, replica_groups=mesh['px'=8,'py'=4] {'px','py'}, use_global_device_ids=true, to_apply=%region_16.17 | all-reduce | flops 1 | bytes 8 | tf_op jit(solution)/shard_map/psum | solution.py:164
  1184.8 38.8 %psum.78 = f32[]{:T(128)} all-reduce(f32[]{:T(128)} %get-tuple-element.6), channel_id=1, replica_groups=mesh['px'=8,'py'=4] {'px','py'}, use_global_device_ids=true, to_apply=%region_18.19 | all-reduce | flops 1 | bytes 8 | tf_op jit(solution)/shard_map/psum | solution.py:122
  1270.8 6.4 all-to-all-done.42
  1328.0 6.3 all-to-all-start.45
  1390.2 6.8 all-to-all-start.48
  1400.7 6.0 all-to-all-done.48
  1415.2 42.0 %psum.79 = f32[]{:T(128)} all-reduce(f32[]{:T(128)} %get-tuple-element.34), channel_id=1, replica_groups=mesh['px'=8,'py'=4] {'px','py'}, use_global_device_ids=true, to_apply=%region_20.21 | all-reduce | flops 1 | bytes 8 | tf_op jit(solution)/shard_map/psum | solution.py:164
  1465.6 7.5 all-to-all-done.50
  1477.5 7.9 all-to-all-done.49
  (505 shorter events, 852.0 us)
Async XLA Ops:
  0.6 13.1 all-to-all-start
  30.6 12.3 all-to-all-start.3
  43.6 21.6 %all-to-all-start.2 = ((f32[8,1,16384]{2,1,0:T(1,128)}), f32[8,1,16384]{2,1,0:T(1,128)S(1)}, u32[]{:S(2)}, u32[]{:S(2)}) async-start(f32[8,1,16384]{2,1,0:T(1,128)} %reshape.82), calls=%async_computation.2 | async-start | bytes 1048576 | tf_op jit(solution)/shard_map/all_to_all | solution.py:91
  65.3 18.7 %all-to-all-start.4 = ((f32[8,1,16384]{2,1,0:T(1,128)}), f32[8,1,16384]{2,1,0:T(1,128)}, u32[]{:S(2)}, u32[]{:S(2)}) async-start(f32[8,1,16384]{2,1,0:T(1,128)} %reshape.84), calls=%async_computation.4 | async-start | bytes 1048576 | tf_op jit(solution)/shard_map/all_to_all | solution.py:92
  103.2 19.9 %all-to-all-start.5 = ((f32[8,1,16384]{2,1,0:T(1,128)}), f32[8,1,16384]{2,1,0:T(1,128)}, u32[]{:S(2)}, u32[]{:S(2)}) async-start(f32[8,1,16384]{2,1,0:T(1,128)} %reshape.86), calls=%async_computation.5 | async-start | bytes 1048576 | tf_op jit(solution)/shard_map/all_to_all | solution.py:98
  123.1 19.0 %all-to-all-start.7 = ((f32[8,1,16384]{2,1,0:T(1,128)}), f32[8,1,16384]{2,1,0:T(1,128)}, u32[]{:S(2)}, u32[]{:S(2)}) async-start(f32[8,1,16384]{2,1,0:T(1,128)} %reshape.88), calls=%async_computation.7 | async-start | bytes 1048576 | tf_op jit(solution)/shard_map/all_to_all | solution.py:99
  142.1 13.0 all-to-all-start.6
  155.1 12.4 all-to-all-start.8
  188.5 13.2 all-to-all-start.11
  201.7 19.0 %all-to-all-start.10 = ((f32[8,1,16384]{2,1,0:T(1,128)}), f32[8,1,16384]{2,1,0:T(1,128)}, u32[]{:S(2)}, u32[]{:S(2)}) async-start(f32[8,1,16384]{2,1,0:T(1,128)} %reshape.90), calls=%async_computation.10 | async-start | bytes 1048576 | tf_op jit(solution)/shard_map/all_to_all | solution.py:91
  220.7 19.0 %all-to-all-start.12 = ((f32[8,1,16384]{2,1,0:T(1,128)}), f32[8,1,16384]{2,1,0:T(1,128)}, u32[]{:S(2)}, u32[]{:S(2)}) async-start(f32[8,1,16384]{2,1,0:T(1,128)} %reshape.92), calls=%async_computation.12 | async-start | bytes 1048576 | tf_op jit(solution)/shard_map/all_to_all | solution.py:92
  260.9 20.3 %all-to-all-start.13 = ((f32[8,1,16384]{2,1,0:T(1,128)}), f32[8,1,16384]{2,1,0:T(1,128)}, u32[]{:S(2)}, u32[]{:S(2)}) async-start(f32[8,1,16384]{2,1,0:T(1,128)} %reshape.94), calls=%async_computation.13 | async-start | bytes 1048576 | tf_op jit(solution)/shard_map/all_to_all | solution.py:98
  281.2 18.7 %all-to-all-start.15 = ((f32[8,1,16384]{2,1,0:T(1,128)}), f32[8,1,16384]{2,1,0:T(1,128)}, u32[]{:S(2)}, u32[]{:S(2)}) async-start(f32[8,1,16384]{2,1,0:T(1,128)} %reshape.96), calls=%async_computation.15 | async-start | bytes 1048576 | tf_op jit(solution)/shard_map/all_to_all | solution.py:99
  299.9 21.0 %all-to-all-start.14 = ((f32[32,32,128]{2,1,0:T(8,128)}), f32[32,32,128]{2,1,0:T(8,128)}, u32[]{:S(2)}, u32[]{:S(2)}) async-start(f32[32,32,128]{2,1,0:T(8,128)} %copy.343), calls=%async_computation.14 | async-start | bytes 1048576 | tf_op jit(solution)/shard_map/all_to_all | solution.py:102
  320.8 16.1 %all-to-all-start.16 = ((f32[32,32,128]{2,1,0:T(8,128)}), f32[32,32,128]{2,1,0:T(8,128)S(1)}, u32[]{:S(2)}, u32[]{:S(2)}) async-start(f32[32,32,128]{2,1,0:T(8,128)} %copy.348), calls=%async_computation.16 | async-start | bytes 1048576 | tf_op jit(solution)/shard_map/all_to_all | solution.py:103
  432.4 13.4 all-to-all-start.17
  445.8 12.3 all-to-all-start.19
  458.0 20.2 %all-to-all-start.18 = ((f32[8,1,16384]{2,1,0:T(1,128)}), f32[8,1,16384]{2,1,0:T(1,128)}, u32[]{:S(2)}, u32[]{:S(2)}) async-start(f32[8,1,16384]{2,1,0:T(1,128)} %reshape.98), calls=%async_computation.18 | async-start | bytes 1048576 | tf_op jit(solution)/shard_map/all_to_all | solution.py:91
  478.2 18.7 %all-to-all-start.20 = ((f32[8,1,16384]{2,1,0:T(1,128)}), f32[8,1,16384]{2,1,0:T(1,128)S(1)}, u32[]{:S(2)}, u32[]{:S(2)}) async-start(f32[8,1,16384]{2,1,0:T(1,128)} %reshape.100), calls=%async_computation.20 | async-start | bytes 1048576 | tf_op jit(solution)/shard_map/all_to_all | solution.py:92
  520.0 21.3 %all-to-all-start.21 = ((f32[8,1,16384]{2,1,0:T(1,128)}), f32[8,1,16384]{2,1,0:T(1,128)}, u32[]{:S(2)}, u32[]{:S(2)}) async-start(f32[8,1,16384]{2,1,0:T(1,128)} %reshape.102), calls=%async_computation.21 | async-start | bytes 1048576 | tf_op jit(solution)/shard_map/all_to_all | solution.py:98
  541.3 18.5 %all-to-all-start.23 = ((f32[8,1,16384]{2,1,0:T(1,128)}), f32[8,1,16384]{2,1,0:T(1,128)S(1)}, u32[]{:S(2)}, u32[]{:S(2)}) async-start(f32[8,1,16384]{2,1,0:T(1,128)} %reshape.104), calls=%async_computation.23 | async-start | bytes 1048576 | tf_op jit(solution)/shard_map/all_to_all | solution.py:99
  559.8 21.0 %all-to-all-start.22 = ((f32[32,32,128]{2,1,0:T(8,128)}), f32[32,32,128]{2,1,0:T(8,128)}, u32[]{:S(2)}, u32[]{:S(2)}) async-start(f32[32,32,128]{2,1,0:T(8,128)} %copy.371), calls=%async_computation.22 | async-start | bytes 1048576 | tf_op jit(solution)/shard_map/all_to_all | solution.py:102
  580.8 17.0 %all-to-all-start.24 = ((f32[32,32,128]{2,1,0:T(8,128)}), f32[32,32,128]{2,1,0:T(8,128)}, u32[]{:S(2)}, u32[]{:S(2)}) async-start(f32[32,32,128]{2,1,0:T(8,128)} %copy.376), calls=%async_computation.24 | async-start | bytes 1048576 | tf_op jit(solution)/shard_map/all_to_all | solution.py:103
  696.0 13.2 all-to-all-start.25
  721.4 20.4 %all-to-all-start.26 = ((f32[8,1,16384]{2,1,0:T(1,128)}), f32[8,1,16384]{2,1,0:T(1,128)}, u32[]{:S(2)}, u32[]{:S(2)}) async-start(f32[8,1,16384]{2,1,0:T(1,128)} %reshape.106), calls=%async_computation.26 | async-start | bytes 1048576 | tf_op jit(solution)/shard_map/all_to_all | solution.py:91
  741.8 18.8 %all-to-all-start.28 = ((f32[8,1,16384]{2,1,0:T(1,128)}), f32[8,1,16384]{2,1,0:T(1,128)S(1)}, u32[]{:S(2)}, u32[]{:S(2)}) async-start(f32[8,1,16384]{2,1,0:T(1,128)} %reshape.108), calls=%async_computation.28 | async-start | bytes 1048576 | tf_op jit(solution)/shard_map/all_to_all | solution.py:92
  784.0 20.6 %all-to-all-start.29 = ((f32[8,1,16384]{2,1,0:T(1,128)}), f32[8,1,16384]{2,1,0:T(1,128)}, u32[]{:S(2)}, u32[]{:S(2)}) async-start(f32[8,1,16384]{2,1,0:T(1,128)} %reshape.110), calls=%async_computation.29 | async-start | bytes 1048576 | tf_op jit(solution)/shard_map/all_to_all | solution.py:98
  804.6 19.0 %all-to-all-start.31 = ((f32[8,1,16384]{2,1,0:T(1,128)}), f32[8,1,16384]{2,1,0:T(1,128)S(1)}, u32[]{:S(2)}, u32[]{:S(2)}) async-start(f32[8,1,16384]{2,1,0:T(1,128)} %reshape.112), calls=%async_computation.31 | async-start | bytes 1048576 | tf_op jit(solution)/shard_map/all_to_all | solution.py:99
  823.5 21.1 %all-to-all-start.30 = ((f32[32,32,128]{2,1,0:T(8,128)}), f32[32,32,128]{2,1,0:T(8,128)}, u32[]{:S(2)}, u32[]{:S(2)}) async-start(f32[32,32,128]{2,1,0:T(8,128)} %copy.399), calls=%async_computation.30 | async-start | bytes 1048576 | tf_op jit(solution)/shard_map/all_to_all | solution.py:102
  844.6 17.0 %all-to-all-start.32 = ((f32[32,32,128]{2,1,0:T(8,128)}), f32[32,32,128]{2,1,0:T(8,128)}, u32[]{:S(2)}, u32[]{:S(2)}) async-start(f32[32,32,128]{2,1,0:T(8,128)} %copy.404), calls=%async_computation.32 | async-start | bytes 1048576 | tf_op jit(solution)/shard_map/all_to_all | solution.py:103
  959.8 13.4 all-to-all-start.33
  973.2 13.0 all-to-all-start.35
  986.2 20.4 %all-to-all-start.34 = ((f32[8,1,16384]{2,1,0:T(1,128)}), f32[8,1,16384]{2,1,0:T(1,128)}, u32[]{:S(2)}, u32[]{:S(2)}) async-start(f32[8,1,16384]{2,1,0:T(1,128)} %reshape.114), calls=%async_computation.34 | async-start | bytes 1048576 | tf_op jit(solution)/shard_map/all_to_all | solution.py:91
  1006.6 19.1 %all-to-all-start.36 = ((f32[8,1,16384]{2,1,0:T(1,128)}), f32[8,1,16384]{2,1,0:T(1,128)}, u32[]{:S(2)}, u32[]{:S(2)}) async-start(f32[8,1,16384]{2,1,0:T(1,128)} %reshape.116), calls=%async_computation.36 | async-start | bytes 1048576 | tf_op jit(solution)/shard_map/all_to_all | solution.py:92
  1052.4 20.5 %all-to-all-start.37 = ((f32[8,1,16384]{2,1,0:T(1,128)}), f32[8,1,16384]{2,1,0:T(1,128)}, u32[]{:S(2)}, u32[]{:S(2)}) async-start(f32[8,1,16384]{2,1,0:T(1,128)} %reshape.118), calls=%async_computation.37 | async-start | bytes 1048576 | tf_op jit(solution)/shard_map/all_to_all | solution.py:98
  1073.0 18.8 %all-to-all-start.39 = ((f32[8,1,16384]{2,1,0:T(1,128)}), f32[8,1,16384]{2,1,0:T(1,128)}, u32[]{:S(2)}, u32[]{:S(2)}) async-start(f32[8,1,16384]{2,1,0:T(1,128)} %reshape.120), calls=%async_computation.39 | async-start | bytes 1048576 | tf_op jit(solution)/shard_map/all_to_all | solution.py:99
  1091.7 22.1 %all-to-all-start.38 = ((f32[32,32,128]{2,1,0:T(8,128)}), f32[32,32,128]{2,1,0:T(8,128)}, u32[]{:S(2)}, u32[]{:S(2)}) async-start(f32[32,32,128]{2,1,0:T(8,128)} %copy.427), calls=%async_computation.38 | async-start | bytes 1048576 | tf_op jit(solution)/shard_map/all_to_all | solution.py:102
  1113.8 16.8 %all-to-all-start.40 = ((f32[32,32,128]{2,1,0:T(8,128)}), f32[32,32,128]{2,1,0:T(8,128)}, u32[]{:S(2)}, u32[]{:S(2)}) async-start(f32[32,32,128]{2,1,0:T(8,128)} %copy.432), calls=%async_computation.40 | async-start | bytes 1048576 | tf_op jit(solution)/shard_map/all_to_all | solution.py:103
  1230.5 13.2 all-to-all-start.41
  1243.7 13.1 all-to-all-start.43
  1256.8 20.5 %all-to-all-start.42 = ((f32[8,1,16384]{2,1,0:T(1,128)}), f32[8,1,16384]{2,1,0:T(1,128)}, u32[]{:S(2)}, u32[]{:S(2)}) async-start(f32[8,1,16384]{2,1,0:T(1,128)} %reshape.122), calls=%async_computation.42 | async-start | bytes 1048576 | tf_op jit(solution)/shard_map/all_to_all | solution.py:91
  1277.3 23.7 %all-to-all-start.44 = ((f32[8,1,16384]{2,1,0:T(1,128)}), f32[8,1,16384]{2,1,0:T(1,128)}, u32[]{:S(2)}, u32[]{:S(2)}) async-start(f32[8,1,16384]{2,1,0:T(1,128)} %reshape.124), calls=%async_computation.44 | async-start | bytes 1048576 | tf_op jit(solution)/shard_map/all_to_all | solution.py:92
  1328.0 21.0 %all-to-all-start.45 = ((f32[8,1,16384]{2,1,0:T(1,128)}), f32[8,1,16384]{2,1,0:T(1,128)}, u32[]{:S(2)}, u32[]{:S(2)}) async-start(f32[8,1,16384]{2,1,0:T(1,128)} %reshape.126), calls=%async_computation.45 | async-start | bytes 1048576 | tf_op jit(solution)/shard_map/all_to_all | solution.py:98
  1349.0 19.1 %all-to-all-start.47 = ((f32[8,1,16384]{2,1,0:T(1,128)}), f32[8,1,16384]{2,1,0:T(1,128)}, u32[]{:S(2)}, u32[]{:S(2)}) async-start(f32[8,1,16384]{2,1,0:T(1,128)} %reshape.128), calls=%async_computation.47 | async-start | bytes 1048576 | tf_op jit(solution)/shard_map/all_to_all | solution.py:99
  1368.1 22.1 %all-to-all-start.46 = ((f32[32,32,128]{2,1,0:T(8,128)}), f32[32,32,128]{2,1,0:T(8,128)}, u32[]{:S(2)}, u32[]{:S(2)}) async-start(f32[32,32,128]{2,1,0:T(8,128)} %copy.455), calls=%async_computation.46 | async-start | bytes 1048576 | tf_op jit(solution)/shard_map/all_to_all | solution.py:102
  1390.2 16.4 %all-to-all-start.48 = ((f32[32,32,128]{2,1,0:T(8,128)}), f32[32,32,128]{2,1,0:T(8,128)}, u32[]{:S(2)}, u32[]{:S(2)}) async-start(f32[32,32,128]{2,1,0:T(8,128)} %copy.460), calls=%async_computation.48 | async-start | bytes 1048576 | tf_op jit(solution)/shard_map/all_to_all | solution.py:103
  1460.7 12.4 all-to-all-start.50
  1473.1 12.3 all-to-all-start.49
  (54 other events, 419.0 us)
where the time goes:
time: 1500 us; the launch traced here: 1490 us
  blocking collectives  365 us (24%)
  local copies, waits for them, and re-layouts  348 us (23%)
  starting transfers between devices  260 us (17%)
  waiting for transfers between devices  215 us (14%)
  matrix products  196 us (13%)
  other arithmetic  87.8 us (6%)
  between operations  15.1 us (1%)
    psum x5, blocking collectives, squares(): return lax.psum(jnp.sum(residual * residual), ('px', 'py'))  197 us
    dot_general x120, matrix products, contract(): return jnp.einsum(form, left, table, precision=highest)  187 us
    psum x4, blocking collectives, shards(): alpha = norm_now / lax.psum(jnp.sum(direction * image), ('px', 'py'))  168 us
    unnamed x130, local copies, waits for them, and re-layouts  112 us
    all_to_all x6, waiting for transfers between devices, spectral(): lax.all_to_all(real_part, 'px', split_axis=2, concat_axis=0, tiled=True)  49 us
    all_to_all x6, starting transfers between devices, spectral(): lax.all_to_all(imag_part, 'py', split_axis=0, concat_axis=1, tiled=True)  38.1 us
    all_to_all x6, waiting for transfers between devices, spectral(): lax.all_to_all(imag_part, 'py', split_axis=0, concat_axis=1, tiled=True)  37.5 us
    all_to_all x6, starting transfers between devices, spectral(): lax.all_to_all(real_part, 'px', split_axis=0, concat_axis=2, tiled=True)  35.9 us
  transfers between devices with their start and end apart: 61, of which 48 were waited for; matrix products, arithmetic and copies ran while one was open for 27% of the time, Pallas kernels for 0%

commit v1 on v0

v1 whole, which is shorter than its diff:
```python
import functools

import jax
import jax.numpy as jnp
import numpy as np
from jax import lax
from jax.experimental import pallas as pl
from jax.experimental.pallas import tpu as pltpu
from jax.sharding import PartitionSpec as P

ITERS = 5
MESH = pl.DeviceIdType.MESH
DIRECTIONS = [(1, 0), (-1, 0), (0, 1), (0, -1), (1, 1), (1, -1), (-1, 1), (-1, -1)]


def round_up(value, unit):
    return -(-value // unit) * unit


def split_table(table):
    table = table.astype(np.float32)
    high = table.astype(jnp.bfloat16)
    low = (table - high.astype(np.float32)).astype(jnp.bfloat16)
    return high, low


def stacked(table):
    high, low = split_table(table)
    return np.concatenate([high, high, low], axis=1)


def make_tables(local_x, local_y, planes, reach_x, reach_y):
    pad_x, pad_y = round_up(reach_x, 8), round_up(reach_y, 8)
    size_x, size_y = local_x + 2 * reach_x, local_y + 2 * reach_y
    ext_x, ext_y = local_x + 2 * pad_x, local_y + 2 * pad_y
    waves_y = round_up(size_y // 2 + 1, 8)

    def forward(ext, size, pad, reach, rows, used):
        spot = np.arange(ext) - (pad - reach)
        inside = (spot >= 0) & (spot < size)
        wave = np.arange(rows)
        angle = 2.0 * np.pi * ((wave[:, None] * spot[None, :]) % size) / size
        mask = inside[None, :] * (wave < used)[:, None]
        return np.cos(angle) * mask, np.sin(angle) * mask

    cos_y, sin_y = forward(ext_y, size_y, pad_y, reach_y, waves_y, size_y // 2 + 1)
    cos_x, sin_x = forward(ext_x, size_x, pad_x, reach_x, ext_x, size_x)
    y_forward = np.concatenate([cos_y, -sin_y], axis=0)
    x_forward = np.concatenate([cos_x, sin_x], axis=0)
    keep_x = slice(pad_x, pad_x + local_x)
    keep_y = slice(pad_y, pad_y + local_y)
    x_inverse = np.concatenate([cos_x[:, keep_x].T, sin_x[:, keep_x].T], axis=0) / size_x
    weight = np.full(waves_y, 2.0)
    weight[0] = 1.0
    if size_y % 2 == 0:
        weight[size_y // 2] = 1.0
    weight = weight[:, None] / size_y
    y_inverse = np.concatenate([(cos_y * weight)[:, keep_y], -(sin_y * weight)[:, keep_y]], axis=0).T
    index = np.arange(planes)
    angle = 2.0 * np.pi * ((index[:, None] * index[None, :]) % planes) / planes
    cos_z, sin_z = np.cos(angle), np.sin(angle)
    z_forward = np.block([[cos_z, -sin_z], [sin_z, cos_z]])
    z_inverse = np.block([[cos_z, sin_z], [-sin_z, cos_z]]) / planes
    lap = (
        6.0
        - 2.0 * np.cos(2.0 * np.pi * np.arange(waves_y) / size_y)[:, None, None]
        - 2.0 * np.cos(2.0 * np.pi * np.arange(ext_x) / size_x)[None, :, None]
        - 2.0 * np.cos(2.0 * np.pi * index / planes)[None, None, :]
    ).reshape(waves_y * ext_x, planes)
    return dict(
        y_forward=stacked(y_forward),
        x_forward=stacked(x_forward),
        x_inverse=stacked(x_inverse),
        y_inverse=stacked(y_inverse),
        z_forward=np.stack(split_table(z_forward)),
        z_inverse=np.stack(split_table(z_inverse)),
        lap=lap.astype(np.float32),
    )


def halves(values):
    high = values.astype(jnp.bfloat16)
    low = (values - high.astype(jnp.float32)).astype(jnp.bfloat16)
    return high, low


def stack_rows(values):
    high, low = halves(values)
    return jnp.concatenate([high, low, high], axis=0)


def dot(left, right):
    return jnp.dot(left, right, preferred_element_type=jnp.float32)


def kernel(
    shape, psf_shape, groups,
    measured, psf, smoothing, y_fwd, x_fwd, x_inv, y_inv, z_fwd, z_inv, lap,
    field, residual,
    blocks, placed, mixed, spectrum, back, image, walk, pull, power, adjoint, sums_y, sums_x,
    send_sem, recv_sem, sum_send, sum_recv,
):
    local_x, local_y, planes = shape
    groups_x, groups_y = groups
    pad_x = (blocks.shape[1] - local_x) // 2
    pad_y = (blocks.shape[2] - local_y) // 2
    ext_x, ext_y = blocks.shape[1], blocks.shape[2]
    waves = y_fwd.shape[0] // 2
    rows = waves * ext_x
    me_x, me_y = lax.axis_index("px"), lax.axis_index("py")
    penalty = smoothing[0]

    def device(step_x, step_y):
        return {
            "px": lax.rem(me_x + step_x + groups_x, groups_x),
            "py": lax.rem(me_y + step_y + groups_y, groups_y),
        }

    barrier = pltpu.get_barrier_semaphore()
    partners = DIRECTIONS + [(0, k) for k in range(1, groups_y)] + [(k, 0) for k in range(1, groups_x)]
    for step in partners:
        pl.semaphore_signal(barrier, inc=1, device_id=device(*step), device_id_type=MESH)

    inner_x, inner_y = pl.ds(pad_x, local_x), pl.ds(pad_y, local_y)

    def span(step, local, pad):
        if step == 0:
            return pl.ds(pad, local), pl.ds(pad, local)
        if step > 0:
            return pl.ds(local, pad), pl.ds(0, pad)
        return pl.ds(pad, pad), pl.ds(pad + local, pad)

    def halo(side):
        copies = []
        for number, (step_x, step_y) in enumerate(DIRECTIONS):
            from_x, to_x = span(step_x, local_x, pad_x)
            from_y, to_y = span(step_y, local_y, pad_y)
            copies.append(
                pltpu.make_async_remote_copy(
                    src_ref=blocks.at[side, from_x, from_y, :],
                    dst_ref=blocks.at[side, to_x, to_y, :],
                    send_sem=send_sem.at[side, number],
                    recv_sem=recv_sem.at[side, number],
                    device_id=device(step_x, step_y),
                    device_id_type=MESH,
                )
            )
        for copy in copies:
            copy.start()
        return copies

    def forward(block):
        @pl.loop(0, ext_x // 8)
        def _(group):
            for k in range(4):
                x = group * 8 + 2 * k
                pair = jnp.concatenate([block[x], block[x + 1]], axis=1)
                out = dot(y_fwd[...], stack_rows(pair))
                mixed[pl.ds(x * 2 * waves, 2 * waves), :] = out[:, :planes]
                mixed[pl.ds((x + 1) * 2 * waves, 2 * waves), :] = out[:, planes:]

        @pl.loop(0, waves // 4)
        def _(group):
            for k in range(4):
                wave = group * 4 + k
                real = mixed[pl.ds(wave, ext_x, stride=2 * waves), :]
                imag = mixed[pl.ds(wave + waves, ext_x, stride=2 * waves), :]
                out = dot(x_fwd[...], stack_rows(jnp.concatenate([real, imag], axis=1)))
                cosine, sine = out[:ext_x], out[ext_x:]
                spectrum[pl.ds(wave * ext_x, ext_x), :planes] = cosine[:, :planes] + sine[:, planes:]
                spectrum[pl.ds(wave * ext_x, ext_x), planes:] = cosine[:, planes:] - sine[:, :planes]

    def along_z(values, table):
        high, low = halves(values)
        return dot(high, table[0]) + dot(low, table[0]) + dot(high, table[1])

    chunk = ext_x * 2

    def apply_filter(by):
        @pl.loop(0, rows // chunk)
        def _(group):
            where = pl.ds(group * chunk, chunk)
            values = along_z(spectrum[where, :], z_fwd)
            real, imag = by(where, values[:, :planes], values[:, planes:])
            spectrum[where, :] = along_z(jnp.concatenate([real, imag], axis=1), z_inv)

    def by_power(where, real, imag):
        return real * power[where, :], imag * power[where, :]

    def by_adjoint(where, real, imag):
        re, im = adjoint[where, :planes], adjoint[where, planes:]
        return real * re + imag * im, imag * re - real * im

    def inverse(store):
        @pl.loop(0, waves // 4)
        def _(group):
            for k in range(4):
                wave = group * 4 + k
                out = dot(x_inv[...], stack_rows(spectrum[pl.ds(wave * ext_x, ext_x), :]))
                cosine, sine = out[:local_x], out[local_x:]
                back[pl.ds(wave * local_x, local_x), :] = cosine[:, :planes] - sine[:, planes:]
                back[pl.ds((wave + waves) * local_x, local_x), :] = cosine[:, planes:] + sine[:, :planes]

        @pl.loop(0, local_x // 8)
        def _(group):
            for k in range(4):
                x = group * 8 + 2 * k
                left = back[pl.ds(x, 2 * waves, stride=local_x), :]
                right = back[pl.ds(x + 1, 2 * waves, stride=local_x), :]
                out = dot(y_inv[...], stack_rows(jnp.concatenate([left, right], axis=1)))
                store(x, out[:, :planes])
                store(x + 1, out[:, planes:])

    def fold(values):
        return jnp.sum(values.reshape(-1, 8, planes), axis=0)

    def total(gamma, delta, side):
        row = lax.broadcasted_iota(jnp.int32, (8, planes), 0)
        tile = jnp.where(
            row == 0,
            jnp.sum(gamma, axis=0, keepdims=True),
            jnp.where(row == 1, jnp.sum(delta, axis=0, keepdims=True), 0.0),
        )
        for slots, mine, count, base in (
            (sums_y, me_y, groups_y, 0),
            (sums_x, me_x, groups_x, groups_y),
        ):
            slots[side, pl.ds(mine, 1)] = tile[None]
            copies = []
            for k in range(1, count):
                copies.append(
                    pltpu.make_async_remote_copy(
                        src_ref=slots.at[side, mine],
                        dst_ref=slots.at[side, mine],
                        send_sem=sum_send.at[side, base + k],
                        recv_sem=sum_recv.at[side, base + k],
                        device_id=device(0, k) if base == 0 else device(k, 0),
                        device_id_type=MESH,
                    )
                )
            for copy in copies:
                copy.start()
            for copy in copies:
                copy.wait_recv()
            tile = jnp.sum(slots[side], axis=0)
            for copy in copies:
                copy.wait_send()
        sums = jnp.sum(tile, axis=1, keepdims=True)
        return sums[0:1], sums[1:2]

    blocks[0, inner_x, inner_y, :] = measured[...]
    placed[...] = jnp.zeros_like(placed)
    count_x, count_y, _ = psf_shape
    unit = psf[...] / jnp.sum(psf[...])
    origin_x, size_x = pad_x - (count_x - 1), local_x + 2 * (count_x - 1)
    origin_y, size_y = pad_y - (count_y - 1), local_y + 2 * (count_y - 1)
    half_x, half_y = count_x // 2, count_y // 2
    for low_x, high_x in ((0, half_x), (half_x, count_x)):
        at_x = origin_x + (low_x - half_x) % size_x
        for low_y, high_y in ((0, half_y), (half_y, count_y)):
            at_y = origin_y + (low_y - half_y) % size_y
            placed[at_x:at_x + high_x - low_x, at_y:at_y + high_y - low_y, :] = unit[low_x:high_x, low_y:high_y]
    pl.semaphore_wait(barrier, len(partners))
    copies = halo(0)
    forward(placed)

    @pl.loop(0, rows // chunk)
    def _(group):
        where = pl.ds(group * chunk, chunk)
        values = along_z(spectrum[where, :], z_fwd)
        adjoint[where, :] = values
        real, imag = values[:, :planes], values[:, planes:]
        power[where, :] = real * real + imag * imag + penalty * lap[where, :]

    for copy in copies:
        copy.wait_recv()
    forward(blocks.at[0])
    apply_filter(by_adjoint)

    def store_right(x, values):
        blocks[1, pad_x + x, inner_y, :] = values

    inverse(store_right)
    for copy in copies:
        copy.wait_send()

    @pl.loop(0, local_x)
    def _(x):
        field[x] = jnp.zeros((local_y, planes), jnp.float32)

    row = lax.broadcasted_iota(jnp.int32, (local_y, planes), 0)
    lane = lax.broadcasted_iota(jnp.int32, (local_y, planes), 1)
    zero = jnp.zeros((1, 1), jnp.float32)
    edge_low_x = jnp.where(me_x == 0, penalty, 0.0)
    edge_high_x = jnp.where(me_x == groups_x - 1, penalty, 0.0)
    face_low_y = jnp.where((row == 0) & (me_y == 0), penalty, 0.0)
    face_high_y = jnp.where((row == local_y - 1) & (me_y == groups_y - 1), penalty, 0.0)
    face_low_z = jnp.where(lane == 0, penalty, 0.0)
    face_high_z = jnp.where(lane == planes - 1, penalty, 0.0)

    alpha_old, gamma_old = None, None
    for count in range(ITERS):
        side = (count + 1) % 2
        copies = halo(side)
        for copy in copies:
            copy.wait_recv()
        forward(blocks.at[side])
        apply_filter(by_power)

        def store_image(x, values):
            image[x] = values

        inverse(store_image)
        image[0] += edge_low_x * blocks[side, pad_x - 1, inner_y, :]
        image[local_x - 1] += edge_high_x * blocks[side, pad_x + local_x, inner_y, :]

        def finish(x, carry):
            gamma, delta = carry
            here = blocks[side, pad_x + x, inner_y, :]
            below = blocks[side, pad_x + x, pl.ds(pad_y - 1, 1), :]
            above = blocks[side, pad_x + x, pl.ds(pad_y + local_y, 1), :]
            value = image[x] + face_low_y * below + face_high_y * above
            value = value + face_low_z * pltpu.roll(here, 1, 1)
            value = value + face_high_z * pltpu.roll(here, planes - 1, 1)
            image[x] = value
            return gamma + fold(here * here), delta + fold(here * value)

        blank = jnp.zeros((8, planes), jnp.float32)
        gamma, delta = total(*lax.fori_loop(0, local_x, finish, (blank, blank)), side)
        for copy in copies:
            copy.wait_send()
        if count == 0:
            beta = zero
            alpha = gamma / delta
        else:
            beta = gamma / gamma_old
            alpha = gamma / (delta - beta * gamma / alpha_old)
        alpha_old, gamma_old = alpha, gamma
        final = count == ITERS - 1

        @pl.loop(0, local_x)
        def _(x):
            here = blocks[side, pad_x + x, inner_y, :]
            if count == 0:
                step, moved = here, image[x]
            else:
                step = here + beta * walk[x]
                moved = image[x] + beta * pull[x]
            field[x] += alpha * step
            after = here - alpha * moved
            if final:
                residual[x] = after
            else:
                walk[x] = step
                pull[x] = moved
                blocks[1 - side, pad_x + x, inner_y, :] = after


def shards(measured, spread_function, smoothing):
    local_x, local_y, planes = measured.shape
    count_x, count_y, count_z = spread_function.shape
    groups_x, groups_y = lax.axis_size("px"), lax.axis_size("py")
    tables = make_tables(local_x, local_y, planes, count_x - 1, count_y - 1)
    pad_x, pad_y = round_up(count_x - 1, 8), round_up(count_y - 1, 8)
    ext_x, ext_y = local_x + 2 * pad_x, local_y + 2 * pad_y
    waves = tables["y_forward"].shape[0] // 2
    along = jnp.pad(spread_function, ((0, 0), (0, 0), (0, planes - count_z)))
    along = jnp.roll(along, -(count_z // 2), axis=2)
    f32 = jnp.float32
    vmem = pl.BlockSpec(memory_space=pltpu.VMEM)
    body = functools.partial(
        kernel, (local_x, local_y, planes), spread_function.shape, (groups_x, groups_y)
    )
    local = (local_x, local_y, planes)
    return pl.pallas_call(
        body,
        out_shape=[jax.ShapeDtypeStruct(local, f32)] * 2,
        in_specs=[vmem, vmem, pl.BlockSpec(memory_space=pltpu.SMEM)] + [vmem] * 7,
        out_specs=[vmem, vmem],
        scratch_shapes=[
            pltpu.VMEM((2, ext_x, ext_y, planes), f32),
            pltpu.VMEM((ext_x, ext_y, planes), f32),
            pltpu.VMEM((ext_x * 2 * waves, planes), f32),
            pltpu.VMEM((waves * ext_x, 2 * planes), f32),
            pltpu.VMEM((2 * waves * local_x, planes), f32),
            pltpu.VMEM(local, f32),
            pltpu.VMEM(local, f32),
            pltpu.VMEM(local, f32),
            pltpu.VMEM((waves * ext_x, planes), f32),
            pltpu.VMEM((waves * ext_x, 2 * planes), f32),
            pltpu.VMEM((2, groups_y, 8, planes), f32),
            pltpu.VMEM((2, groups_x, 8, planes), f32),
            pltpu.SemaphoreType.DMA((2, len(DIRECTIONS))),
            pltpu.SemaphoreType.DMA((2, len(DIRECTIONS))),
            pltpu.SemaphoreType.DMA((2, groups_x + groups_y)),
            pltpu.SemaphoreType.DMA((2, groups_x + groups_y)),
        ],
        compiler_params=pltpu.CompilerParams(
            collective_id=0, has_side_effects=True, vmem_limit_bytes=48 * 1024 * 1024
        ),
    )(
        measured, along, smoothing,
        *[jnp.asarray(tables[name]) for name in (
            "y_forward", "x_forward", "x_inverse", "y_inverse", "z_forward", "z_inverse", "lap"
        )],
    )


def solution(mesh):
    return jax.shard_map(
        shards,
        mesh=mesh,
        in_specs=(P("px", "py", None), P(), P()),
        out_specs=(P("px", "py", None), P("px", "py", None)),
        check_vma=False,
    )
```

time: 1500 us -> 184 us (0.12)
  blocking collectives: 365 us -> 0 us
  local copies, waits for them, and re-layouts: 348 us -> 7.2 us
  starting transfers between devices: 260 us -> 0 us
  waiting for transfers between devices: 215 us -> 0 us
  matrix products: 196 us -> 0 us
  Pallas kernels: 0 us -> 175 us
  other arithmetic: 87.8 us -> 0.08 us
    psum x9 -> x0, blocking collectives: 365 us -> none  [the longest x5 197 us: squares(): return lax.psum(jnp.sum(residual * residual), ('px', 'py'))]
    all_to_all x51 -> x0, starting transfers between devices: 238 us -> none  [the longest x6 38.1 us: spectral(): lax.all_to_all(imag_part, 'py', split_axis=0, concat_axis=1, tiled=True)]
    all_to_all x51 -> x0, waiting for transfers between devices: 211 us -> none  [the longest x6 49 us: spectral(): lax.all_to_all(real_part, 'px', split_axis=2, concat_axis=0, tiled=True)]
    dot_general x130 -> x0, matrix products: 196 us -> none  [the longest x120 187 us: contract(): return jnp.einsum(form, left, table, precision=highest)]
    all_to_all x88 -> x0, local copies, waits for them, and re-layouts: 188 us -> none  [the longest x12 34.1 us: spectral(): lax.all_to_all(imag_part, 'px', split_axis=0, concat_axis=2, tiled=True)]
    pallas_call x0 -> x1, Pallas kernels: none -> 175 us  [shards(): pl.pallas_call(body, out_shape=[jax.ShapeDtypeStruct(local, f32)] * 2, in...]
    unnamed x130 -> x20, local copies, waits for them, and re-layouts: 112 us -> 6.31 us
    all_to_all x24 -> x0, other arithmetic: 69.3 us -> none  [the longest x6 18.2 us: spectral(): lax.all_to_all(real_part, 'px', split_axis=0, concat_axis=2, tiled=True)]
  transfers between devices with their start and end apart: 61 -> 0, of which waited for: 48 -> 0; matrix products, arithmetic and copies ran while one was open for 27% -> 0% of each run, Pallas kernels for 0% -> 0%
where the time goes in v1:
time: 184 us
  Pallas kernels  175 us (95%)
  local copies, waits for them, and re-layouts  7.2 us (4%)
    pallas_call x1, Pallas kernels, shards(): pl.pallas_call(body, out_shape=[jax.ShapeDtypeStruct(local, f32)] * 2, in...  175 us
    unnamed x20, local copies, waits for them, and re-layouts  6.31 us

profile of v1, /device:TPU:0, one launch (start us, length us, event | category | flops | bytes accessed | tf_op | source)
XLA Modules:
  0.0 183.6 jit_solution(2241812545846887163)
XLA Ops:
  1.3 0.0 copy-start.8
  1.3 0.0 copy-start.6
  1.3 0.9 pad_slice_fusion
  2.2 0.0 copy-done.8
  2.2 0.0 copy-start.4
  2.2 0.0 copy-start.5
  2.2 0.0 copy-start.7
  2.2 0.1 pad_maximum_fusion.psf
  2.3 0.0 copy-done.6
  2.3 0.7 copy-done.4
  3.0 0.0 copy-done.5
  3.0 0.0 copy-done.7
  3.0 0.0 copy-start
  3.0 1.1 copy-done
  4.1 0.0 copy-start.1
  4.1 1.0 copy-done.1
  5.1 0.0 copy-start.2
  5.1 0.9 copy-done.2
  6.1 0.0 copy-start.3
  6.1 0.9 copy-done.3
  7.0 175.0 %shard_map.113 = (f32[32,32,128]{2,1,0:T(8,128)S(1)}, f32[32,32,128]{2,1,0:T(8,128)S(1)}) custom-call(f32[32,32,128]{2,1,0:T(8,128)S(1)} %copy-done.1, f32[8,8,128]{2,1,0:T(8,128)S(1)} %pad_maximum_fusion.psf, f32[1]{0:T(128)S(6)} %copy.14.smoothing, bf16[48,144]{1,0:T(8,128)(2,1)S(1)} %copy-done.6, bf16[96,144]{1,0:T(8,128)(2,1)S(1)} %copy-done.4, ...), custom_call_target="tpu_custom_call" | custom-call | tf_op jit(solution)/shard_map/pallas_call | solution.py:375
  182.0 0.8 copy.15
  182.8 0.8 copy.16
Async XLA Ops:
  1.3 0.9 copy-start.8
  1.3 1.0 copy-start.6
  2.2 0.8 copy-start.4
  2.2 0.8 copy-start.5
  2.2 0.8 copy-start.7
  3.0 1.1 copy-start
  4.1 1.0 copy-start.1
  5.1 0.9 copy-start.2
  6.1 0.9 copy-start.3

commit v2 on v1

--- a/solution.py
+++ b/solution.py
@@ -26,7 +26,7 @@
 
 def stacked(table):
     high, low = split_table(table)
-    return np.concatenate([high, high, low], axis=1)
+    return np.concatenate([high, low, high, low, high], axis=1)
 
 
 def make_tables(local_x, local_y, planes, reach_x, reach_y):
@@ -78,15 +78,16 @@
     )
 
 
-def halves(values):
+def thirds(values):
     high = values.astype(jnp.bfloat16)
-    low = (values - high.astype(jnp.float32)).astype(jnp.bfloat16)
-    return high, low
+    rest = values - high.astype(jnp.float32)
+    middle = rest.astype(jnp.bfloat16)
+    return high, middle, (rest - middle.astype(jnp.float32)).astype(jnp.bfloat16)
 
 
 def stack_rows(values):
-    high, low = halves(values)
-    return jnp.concatenate([high, low, high], axis=0)
+    high, middle, low = thirds(values)
+    return jnp.concatenate([high, high, middle, middle, low], axis=0)
 
 
 def dot(left, right):
@@ -95,10 +96,11 @@
 
 def kernel(
     shape, psf_shape, groups,
-    measured, psf, smoothing, y_fwd, x_fwd, x_inv, y_inv, z_fwd, z_inv, lap,
+    measured, psf, smoothing, y_fwd, x_fwd, x_inv, y_inv, z_fwd_far, z_inv_far, lap_far,
     field, residual,
     blocks, placed, mixed, spectrum, back, image, walk, pull, power, adjoint, sums_y, sums_x,
-    send_sem, recv_sem, sum_send, sum_recv,
+    swing, unit, z_fwd, z_inv, lap,
+    send_sem, recv_sem, sum_send, sum_recv, load_sem,
 ):
     local_x, local_y, planes = shape
     groups_x, groups_y = groups
@@ -109,6 +111,8 @@
     rows = waves * ext_x
     me_x, me_y = lax.axis_index("px"), lax.axis_index("py")
     penalty = smoothing[0]
+    count_x, count_y, count_z = psf_shape
+    reach_x = count_x - 1
 
     def device(step_x, step_y):
         return {
@@ -122,19 +126,30 @@
         pl.semaphore_signal(barrier, inc=1, device_id=device(*step), device_id_type=MESH)
 
     inner_x, inner_y = pl.ds(pad_x, local_x), pl.ds(pad_y, local_y)
-
-    def span(step, local, pad):
+    loads = [
+        pltpu.make_async_copy(far, near, load_sem.at[number])
+        for number, (far, near) in enumerate((
+            (measured, blocks.at[0, inner_x, inner_y, :]),
+            (z_fwd_far, z_fwd), (lap_far, lap), (z_inv_far, z_inv),
+        ))
+    ]
+    for load in loads:
+        load.start()
+
+    def span(step, local, pad, width):
         if step == 0:
             return pl.ds(pad, local), pl.ds(pad, local)
         if step > 0:
-            return pl.ds(local, pad), pl.ds(0, pad)
-        return pl.ds(pad, pad), pl.ds(pad + local, pad)
-
-    def halo(side):
+            return pl.ds(pad + local - width, width), pl.ds(pad - width, width)
+        return pl.ds(pad, width), pl.ds(pad + local, width)
+
+    def halo(side, across):
         copies = []
         for number, (step_x, step_y) in enumerate(DIRECTIONS):
-            from_x, to_x = span(step_x, local_x, pad_x)
-            from_y, to_y = span(step_y, local_y, pad_y)
+            if (step_x != 0) != across:
+                continue
+            from_x, to_x = span(step_x, local_x, pad_x, reach_x)
+            from_y, to_y = span(step_y, local_y, pad_y, pad_y)
             copies.append(
                 pltpu.make_async_remote_copy(
                     src_ref=blocks.at[side, from_x, from_y, :],
@@ -149,15 +164,23 @@
             copy.start()
         return copies
 
-    def forward(block):
-        @pl.loop(0, ext_x // 8)
-        def _(group):
+    def forward(block, beside=(), across=()):
+        def lines(group):
             for k in range(4):
                 x = group * 8 + 2 * k
                 pair = jnp.concatenate([block[x], block[x + 1]], axis=1)
                 out = dot(y_fwd[...], stack_rows(pair))
                 mixed[pl.ds(x * 2 * waves, 2 * waves), :] = out[:, :planes]
                 mixed[pl.ds((x + 1) * 2 * waves, 2 * waves), :] = out[:, planes:]
+
+        for copy in beside:
+            copy.wait_recv()
+        pl.loop(pad_x // 8, (pad_x + local_x) // 8)(lines)
+        for copy in across:
+            copy.wait_recv()
+        edge = pad_x // 8
+        pl.loop(0, edge)(lines)
+        pl.loop(ext_x // 8 - edge, ext_x // 8)(lines)
 
         @pl.loop(0, waves // 4)
         def _(group):
@@ -171,10 +194,11 @@
                 spectrum[pl.ds(wave * ext_x, ext_x), planes:] = cosine[:, planes:] - sine[:, :planes]
 
     def along_z(values, table):
-        high, low = halves(values)
-        return dot(high, table[0]) + dot(low, table[0]) + dot(high, table[1])
-
-    chunk = ext_x * 2
+        high, middle, low = thirds(values)
+        small = dot(low, table[0]) + dot(middle, table[1])
+        return dot(high, table[0]) + (dot(middle, table[0]) + dot(high, table[1]) + small)
+
+    chunk = rows // 2
 
     def apply_filter(by):
         @pl.loop(0, rows // chunk)
@@ -211,58 +235,65 @@
                 store(x, out[:, :planes])
                 store(x + 1, out[:, planes:])
 
+    def start_sum(slots, tile, mine, count, base, side):
+        slots[side, pl.ds(mine, 1)] = tile[None]
+        copies = []
+        for k in range(1, count):
+            copies.append(
+                pltpu.make_async_remote_copy(
+                    src_ref=slots.at[side, mine],
+                    dst_ref=slots.at[side, mine],
+                    send_sem=sum_send.at[side, base + k],
+                    recv_sem=sum_recv.at[side, base + k],
+                    device_id=device(0, k) if base == 0 else device(k, 0),
+                    device_id_type=MESH,
+                )
+            )
+        for copy in copies:
+            copy.start()
+        return copies
+
+    def end_sum(slots, copies, side):
+        for copy in copies:
+            copy.wait_recv()
+        tile = jnp.sum(slots[side], axis=0)
+        for copy in copies:
+            copy.wait_send()
+        return tile
+
     def fold(values):
         return jnp.sum(values.reshape(-1, 8, planes), axis=0)
 
-    def total(gamma, delta, side):
-        row = lax.broadcasted_iota(jnp.int32, (8, planes), 0)
-        tile = jnp.where(
-            row == 0,
+    def pack(gamma, delta):
+        line = lax.broadcasted_iota(jnp.int32, (8, planes), 0)
+        return jnp.where(
+            line == 0,
             jnp.sum(gamma, axis=0, keepdims=True),
-            jnp.where(row == 1, jnp.sum(delta, axis=0, keepdims=True), 0.0),
+            jnp.where(line == 1, jnp.sum(delta, axis=0, keepdims=True), 0.0),
         )
-        for slots, mine, count, base in (
-            (sums_y, me_y, groups_y, 0),
-            (sums_x, me_x, groups_x, groups_y),
-        ):
-            slots[side, pl.ds(mine, 1)] = tile[None]
-            copies = []
-            for k in range(1, count):
-                copies.append(
-                    pltpu.make_async_remote_copy(
-                        src_ref=slots.at[side, mine],
-                        dst_ref=slots.at[side, mine],
-                        send_sem=sum_send.at[side, base + k],
-                        recv_sem=sum_recv.at[side, base + k],
-                        device_id=device(0, k) if base == 0 else device(k, 0),
-                        device_id_type=MESH,
-                    )
-                )
-            for copy in copies:
-                copy.start()
-            for copy in copies:
-                copy.wait_recv()
-            tile = jnp.sum(slots[side], axis=0)
-            for copy in copies:
-                copy.wait_send()
-        sums = jnp.sum(tile, axis=1, keepdims=True)
-        return sums[0:1], sums[1:2]
-
-    blocks[0, inner_x, inner_y, :] = measured[...]
+
     placed[...] = jnp.zeros_like(placed)
-    count_x, count_y, _ = psf_shape
-    unit = psf[...] / jnp.sum(psf[...])
+    for side in range(2):
+        blocks[side, 0:pad_x - reach_x] = jnp.zeros((pad_x - reach_x, ext_y, planes), jnp.float32)
+        blocks[side, ext_x - pad_x + reach_x:ext_x] = jnp.zeros((pad_x - reach_x, ext_y, planes), jnp.float32)
+    unit[...] = jnp.zeros_like(unit)
+    unit[:, :, 0:count_z] = psf[...] / jnp.sum(psf[...])
     origin_x, size_x = pad_x - (count_x - 1), local_x + 2 * (count_x - 1)
     origin_y, size_y = pad_y - (count_y - 1), local_y + 2 * (count_y - 1)
     half_x, half_y = count_x // 2, count_y // 2
-    for low_x, high_x in ((0, half_x), (half_x, count_x)):
+    for low_x in range(count_x):
         at_x = origin_x + (low_x - half_x) % size_x
+        turned = pltpu.roll(unit[low_x], planes - count_z // 2, 1)
         for low_y, high_y in ((0, half_y), (half_y, count_y)):
             at_y = origin_y + (low_y - half_y) % size_y
-            placed[at_x:at_x + high_x - low_x, at_y:at_y + high_y - low_y, :] = unit[low_x:high_x, low_y:high_y]
+            placed[at_x, at_y:at_y + high_y - low_y, :] = turned[low_y:high_y]
     pl.semaphore_wait(barrier, len(partners))
-    copies = halo(0)
+    loads[0].wait()
+    across = halo(0, True)
+    beside = halo(0, False)
     forward(placed)
+    loads[1].wait()
+    loads[2].wait()
 
     @pl.loop(0, rows // chunk)
     def _(group):
@@ -272,25 +303,22 @@
         real, imag = values[:, :planes], values[:, planes:]
         power[where, :] = real * real + imag * imag + penalty * lap[where, :]
 
-    for copy in copies:
-        copy.wait_recv()
-    forward(blocks.at[0])
+    loads[3].wait()
+    forward(blocks.at[0], beside, across)
     apply_filter(by_adjoint)
 
     def store_right(x, values):
         blocks[1, pad_x + x, inner_y, :] = values
+        residual[x] = values
 
     inverse(store_right)
-    for copy in copies:
+    for copy in across + beside:
         copy.wait_send()
-
-    @pl.loop(0, local_x)
-    def _(x):
-        field[x] = jnp.zeros((local_y, planes), jnp.float32)
+    across = halo(1, True)
+    beside = halo(1, False)
 
     row = lax.broadcasted_iota(jnp.int32, (local_y, planes), 0)
     lane = lax.broadcasted_iota(jnp.int32, (local_y, planes), 1)
-    zero = jnp.zeros((1, 1), jnp.float32)
     edge_low_x = jnp.where(me_x == 0, penalty, 0.0)
     edge_high_x = jnp.where(me_x == groups_x - 1, penalty, 0.0)
     face_low_y = jnp.where((row == 0) & (me_y == 0), penalty, 0.0)
@@ -298,13 +326,8 @@
     face_low_z = jnp.where(lane == 0, penalty, 0.0)
     face_high_z = jnp.where(lane == planes - 1, penalty, 0.0)
 
-    alpha_old, gamma_old = None, None
-    for count in range(ITERS):
-        side = (count + 1) % 2
-        copies = halo(side)
-        for copy in copies:
-            copy.wait_recv()
-        forward(blocks.at[side])
+    def operate(side, beside, across):
+        forward(blocks.at[side], beside, across)
         apply_filter(by_power)
 
         def store_image(x, values):
@@ -313,47 +336,96 @@
         inverse(store_image)
         image[0] += edge_low_x * blocks[side, pad_x - 1, inner_y, :]
         image[local_x - 1] += edge_high_x * blocks[side, pad_x + local_x, inner_y, :]
-
-        def finish(x, carry):
-            gamma, delta = carry
-            here = blocks[side, pad_x + x, inner_y, :]
-            below = blocks[side, pad_x + x, pl.ds(pad_y - 1, 1), :]
-            above = blocks[side, pad_x + x, pl.ds(pad_y + local_y, 1), :]
-            value = image[x] + face_low_y * below + face_high_y * above
-            value = value + face_low_z * pltpu.roll(here, 1, 1)
-            value = value + face_high_z * pltpu.roll(here, planes - 1, 1)
-            image[x] = value
-            return gamma + fold(here * here), delta + fold(here * value)
-
+        for copy in beside + across:
+            copy.wait_send()
+
+    def faced(side, x, here):
+        below = blocks[side, pad_x + x, pl.ds(pad_y - 1, 1), :]
+        above = blocks[side, pad_x + x, pl.ds(pad_y + local_y, 1), :]
+        value = image[x] + face_low_y * below + face_high_y * above
+        value = value + face_low_z * pltpu.roll(here, 1, 1)
+        return value + face_high_z * pltpu.roll(here, planes - 1, 1)
+
+    def sweep(low, high, line, carry):
+        def some(group, carry):
+            for k in range(4):
+                carry = line(low + group * 4 + k, carry)
+            return carry
+
+        return lax.fori_loop(0, (high - low) // 4, some, carry)
+
+    def sweep_and_send(line, side):
         blank = jnp.zeros((8, planes), jnp.float32)
-        gamma, delta = total(*lax.fori_loop(0, local_x, finish, (blank, blank)), side)
-        for copy in copies:
-            copy.wait_send()
+        carry = sweep(0, pad_x, line, (blank, blank))
+        carry = sweep(local_x - pad_x, local_x, line, carry)
+        across = halo(side, True)
+        carry = sweep(pad_x, local_x - pad_x, line, carry)
+        return pack(*carry), across, halo(side, False)
+
+    operate(1, beside, across)
+
+    def first(x, carry):
+        gamma, delta = carry
+        here = blocks[1, pad_x + x, inner_y, :]
+        value = faced(1, x, here)
+        blocks[0, pad_x + x, inner_y, :] = value
+        return gamma + fold(here * here), delta + fold(here * value)
+
+    tile, across, beside = sweep_and_send(first, 0)
+
+    alpha_old, gamma_old = None, None
+    for count in range(ITERS):
+        side = count % 2
+        final = count == ITERS - 1
+        copies = start_sum(sums_y, tile, me_y, groups_y, 0, side)
+        tile = end_sum(sums_y, copies, side)
+        copies = start_sum(sums_x, tile, me_x, groups_x, groups_y, side)
+        if not final:
+            operate(side, beside, across)
+        sums = jnp.sum(end_sum(sums_x, copies, side), axis=1, keepdims=True)
+        gamma, delta = sums[0:1], sums[1:2]
         if count == 0:
-            beta = zero
+            beta = jnp.zeros((1, 1), jnp.float32)
             alpha = gamma / delta
         else:
             beta = gamma / gamma_old
             alpha = gamma / (delta - beta * gamma / alpha_old)
         alpha_old, gamma_old = alpha, gamma
-        final = count == ITERS - 1
-
-        @pl.loop(0, local_x)
-        def _(x):
-            here = blocks[side, pad_x + x, inner_y, :]
+        alpha_all = jnp.broadcast_to(alpha, (local_y, planes))
+        beta_all = jnp.broadcast_to(beta, (local_y, planes))
+
+        def line(x, carry):
+            held = blocks[side, pad_x + x, inner_y, :]
+            here = residual[x]
             if count == 0:
-                step, moved = here, image[x]
+                step, moved = here, held
+                field[x] = alpha_all * step
             else:
-                step = here + beta * walk[x]
-                moved = image[x] + beta * pull[x]
-            field[x] += alpha * step
-            after = here - alpha * moved
+                step = here + beta_all * walk[x]
+                moved = held + beta_all * pull[x]
+                field[x] += alpha_all * step
+            after = here - alpha_all * moved
+            residual[x] = after
             if final:
-                residual[x] = after
-            else:
-                walk[x] = step
-                pull[x] = moved
-                blocks[1 - side, pad_x + x, inner_y, :] = after
+                return carry
+            walk[x] = step
+            pull[x] = moved
+            turn = faced(side, x, held)
+            if count > 0:
+                turn = turn + beta_all * swing[x]
+            swing[x] = turn
+            value = held - alpha_all * turn
+            blocks[1 - side, pad_x + x, inner_y, :] = value
+            gamma, delta = carry
+            return gamma + fold(after * after), delta + fold(after * value)
+
+        if final:
+            sweep(0, local_x, line, 0)
+        elif count == ITERS - 2:
+            blank = jnp.zeros((8, planes), jnp.float32)
+            tile = pack(*sweep(0, local_x, line, (blank, blank)))
+        else:
+            tile, across, beside = sweep_and_send(line, 1 - side)
 
 
 def shards(measured, spread_function, smoothing):
@@ -364,10 +436,9 @@
     pad_x, pad_y = round_up(count_x - 1, 8), round_up(count_y - 1, 8)
     ext_x, ext_y = local_x + 2 * pad_x, local_y + 2 * pad_y
     waves = tables["y_forward"].shape[0] // 2
-    along = jnp.pad(spread_function, ((0, 0), (0, 0), (0, planes - count_z)))
-    along = jnp.roll(along, -(count_z // 2), axis=2)
     f32 = jnp.float32
     vmem = pl.BlockSpec(memory_space=pltpu.VMEM)
+    far = pl.BlockSpec(memory_space=pltpu.HBM)
     body = functools.partial(
         kernel, (local_x, local_y, planes), spread_function.shape, (groups_x, groups_y)
     )
@@ -375,7 +446,7 @@
     return pl.pallas_call(
         body,
         out_shape=[jax.ShapeDtypeStruct(local, f32)] * 2,
-        in_specs=[vmem, vmem, pl.BlockSpec(memory_space=pltpu.SMEM)] + [vmem] * 7,
+        in_specs=[far, vmem, pl.BlockSpec(memory_space=pltpu.SMEM)] + [vmem] * 4 + [far] * 3,
         out_specs=[vmem, vmem],
         scratch_shapes=[
             pltpu.VMEM((2, ext_x, ext_y, planes), f32),
@@ -390,16 +461,22 @@
             pltpu.VMEM((waves * ext_x, 2 * planes), f32),
             pltpu.VMEM((2, groups_y, 8, planes), f32),
             pltpu.VMEM((2, groups_x, 8, planes), f32),
+            pltpu.VMEM(local, f32),
+            pltpu.VMEM((count_x, count_y, planes), f32),
+            pltpu.VMEM(tables["z_forward"].shape, jnp.bfloat16),
+            pltpu.VMEM(tables["z_inverse"].shape, jnp.bfloat16),
+            pltpu.VMEM(tables["lap"].shape, f32),
             pltpu.SemaphoreType.DMA((2, len(DIRECTIONS))),
             pltpu.SemaphoreType.DMA((2, len(DIRECTIONS))),
             pltpu.SemaphoreType.DMA((2, groups_x + groups_y)),
             pltpu.SemaphoreType.DMA((2, groups_x + groups_y)),
+            pltpu.SemaphoreType.DMA((4,)),
         ],
         compiler_params=pltpu.CompilerParams(
             collective_id=0, has_side_effects=True, vmem_limit_bytes=48 * 1024 * 1024
         ),
     )(
-        measured, along, smoothing,
+        measured, spread_function, smoothing,
         *[jnp.asarray(tables[name]) for name in (
             "y_forward", "x_forward", "x_inverse", "y_inverse", "z_forward", "z_inverse", "lap"
         )],

time: 184 us -> 126 us (0.68)
  Pallas kernels: 175 us -> 114 us
  local copies, waits for them, and re-layouts: 7.2 us -> 9.35 us
    pallas_call x1, Pallas kernels: 175 us -> 114 us  [shards(): pl.pallas_call(body, out_shape=[jax.ShapeDtypeStruct(local, f32)] * 2, in...]
    unnamed x20, local copies, waits for them, and re-layouts: 6.31 us -> 9.35 us
where the time goes in v2:
time: 126 us; the launch traced here: 125 us
  Pallas kernels  114 us (90%)
  local copies, waits for them, and re-layouts  9.35 us (7%)
  between operations  1.3 us (1%)
    pallas_call x1, Pallas kernels, shards(): pl.pallas_call(body, out_shape=[jax.ShapeDtypeStruct(local, f32)] * 2, in...  114 us
    unnamed x20, local copies, waits for them, and re-layouts  9.35 us

profile of v2, /device:TPU:0, one launch (start us, length us, event | category | flops | bytes accessed | tf_op | source)
XLA Modules:
  0.0 125.0 jit_solution(5830002181008908185)
XLA Ops:
  1.3 0.0 copy-start
  1.3 1.1 copy-done
  2.3 0.0 copy-start.1
  2.3 1.0 copy-done.1
  3.4 0.0 copy-start.2
  3.4 0.9 copy-done.2
  4.3 0.0 copy-start.3
  4.3 0.9 copy-done.3
  5.3 0.0 copy-start.4
  5.3 0.8 copy-done.4
  6.1 0.0 copy-start.5
  6.1 0.8 copy-done.5
  6.8 0.0 copy-start.6
  6.8 0.8 copy-done.6
  7.6 0.0 copy-start.7
  7.6 0.7 copy-done.7
  8.3 0.0 copy-start.8
  8.3 0.7 copy-done.8
  9.1 114.3 %shard_map.113 = (f32[32,32,128]{2,1,0:T(8,128)S(1)}, f32[32,32,128]{2,1,0:T(8,128)S(1)}) custom-call(f32[32,32,128]{2,1,0:T(8,128)S(1)} %copy-done.1, f32[8,8,16]{2,1,0:T(8,128)S(1)} %copy-done.5, f32[1]{0:T(128)S(6)} %copy.14.smoothing, bf16[48,240]{1,0:T(8,128)(2,1)S(1)} %copy-done.7, bf16[96,240]{1,0:T(8,128)(2,1)S(1)} %copy-done.4, ...), custom_call_target="tpu_custom_call" | custom-call | tf_op jit(solution)/shard_map/pallas_call | solution.py:446
  123.4 0.8 copy.15
  124.2 0.8 copy.16
Async XLA Ops:
  1.3 1.1 copy-start
  2.3 1.0 copy-start.1
  3.4 0.9 copy-start.2
  4.3 0.9 copy-start.3
  5.3 0.8 copy-start.4
  6.1 0.8 copy-start.5
  6.8 0.8 copy-start.6
  7.6 0.7 copy-start.7
  8.3 0.7 copy-start.8

commit v3 on v2

--- a/solution.py
+++ b/solution.py
@@ -195,8 +195,8 @@
 
     def along_z(values, table):
         high, middle, low = thirds(values)
-        small = dot(low, table[0]) + dot(middle, table[1])
-        return dot(high, table[0]) + (dot(middle, table[0]) + dot(high, table[1]) + small)
+        small = dot(low, table[0]) + dot(high, table[1])
+        return dot(high, table[0]) + (dot(middle, table[0]) + small)
 
     chunk = rows // 2
 

time: 126 us -> 122 us (0.968)
  Pallas kernels: 114 us -> 111 us
    pallas_call x1, Pallas kernels: 114 us -> 111 us  [shards(): pl.pallas_call(body, out_shape=[jax.ShapeDtypeStruct(local, f32)] * 2, in...]
where the time goes in v3:
time: 122 us; the launch traced here: 121 us
  Pallas kernels  111 us (91%)
  local copies, waits for them, and re-layouts  9.35 us (8%)
  between operations  1.3 us (1%)
    pallas_call x1, Pallas kernels, shards(): pl.pallas_call(body, out_shape=[jax.ShapeDtypeStruct(local, f32)] * 2, in...  111 us
    unnamed x20, local copies, waits for them, and re-layouts  9.35 us

profile of v3, /device:TPU:0, one launch (start us, length us, event | category | flops | bytes accessed | tf_op | source)
XLA Modules:
  0.0 121.3 jit_solution(11477696206132067402)
XLA Ops:
  1.3 0.0 copy-start
  1.3 1.1 copy-done
  2.3 0.0 copy-start.1
  2.3 1.0 copy-done.1
  3.4 0.0 copy-start.2
  3.4 0.9 copy-done.2
  4.3 0.0 copy-start.3
  4.3 0.9 copy-done.3
  5.3 0.0 copy-start.4
  5.3 0.8 copy-done.4
  6.1 0.0 copy-start.5
  6.1 0.8 copy-done.5
  6.8 0.0 copy-start.6
  6.8 0.8 copy-done.6
  7.6 0.0 copy-start.7
  7.6 0.7 copy-done.7
  8.3 0.0 copy-start.8
  8.3 0.7 copy-done.8
  9.1 110.6 %shard_map.113 = (f32[32,32,128]{2,1,0:T(8,128)S(1)}, f32[32,32,128]{2,1,0:T(8,128)S(1)}) custom-call(f32[32,32,128]{2,1,0:T(8,128)S(1)} %copy-done.1, f32[8,8,16]{2,1,0:T(8,128)S(1)} %copy-done.5, f32[1]{0:T(128)S(6)} %copy.14.smoothing, bf16[48,240]{1,0:T(8,128)(2,1)S(1)} %copy-done.7, bf16[96,240]{1,0:T(8,128)(2,1)S(1)} %copy-done.4, ...), custom_call_target="tpu_custom_call" | custom-call | tf_op jit(solution)/shard_map/pallas_call | solution.py:446
  119.7 0.8 copy.15
  120.5 0.8 copy.16
Async XLA Ops:
  1.3 1.1 copy-start
  2.3 1.0 copy-start.1
  3.4 0.9 copy-start.2
  4.3 0.9 copy-start.3
  5.3 0.8 copy-start.4
  6.1 0.8 copy-start.5
  6.8 0.8 copy-start.6
  7.6 0.7 copy-start.7
  8.3 0.7 copy-start.8
